TPU v7x, 512 devices: a whole 4x8x8 slice. The times are simulated.
512 devices in a mesh: dp: 4 (over x), ep: 128 (over z, y, core).
Axes of the slice: x: 4, y: 8, z: 8, core: 2. Of those that a mesh axis runs over, the one named last changes fastest.
Arguments:
- tokens: bfloat16 [128, 16, 2048], P('ep', 'dp'), may hold values from -6 to 6
- dest_ids: int32 [128, 16, 8], P('ep', 'dp'), may hold values from 0 to 127, all different within a row; in each aligned block of 16 rows (0 to 15, 16 to 31, ..., all dimensions but the last counted through in order) at most 2 rows name the same one
- gate_fixed: int32 [128, 16, 8], P('ep', 'dp'), may hold values from 1 to 65535
- gate_up: bfloat16 [128, 2, 768, 2048], P('ep', None, 'dp'), may hold values from -0.125 to 0.125
- down: bfloat16 [128, 768, 2048], P('ep', 'dp'), may hold values from -0.21875 to 0.21875
Outputs:
- mixed: bfloat16 [128, 16, 2048], P('ep', 'dp')
Inputs may be any that keep to these rules, and one draw needn't show every extreme that they name: `dest_ids`: each row names 8 different experts; within one column's 16 rows no expert is named by more than 2 routes.
All inputs are finite; a program needn't handle non-finite values.
Results may differ from a plain program's by a relative error of at most 0.012.
Values may be sent and summed in bfloat16 or wider, within the bound.
A program may use at most 192 MiB of HBM per device.

v0:
```python
import jax
import jax.numpy as jnp
from jax import lax
from jax.sharding import PartitionSpec as P


def feed_forward(rows, pair, lower):
    gate = jnp.einsum("nd,hd->nh", rows, pair[0], preferred_element_type=jnp.float32)
    upper = jnp.einsum("nd,hd->nh", rows, pair[1], preferred_element_type=jnp.float32)
    hidden = (jax.nn.silu(gate) * upper).astype(jnp.bfloat16)
    return jnp.dot(hidden, lower, preferred_element_type=jnp.float32).astype(jnp.bfloat16)


def per_device(tokens, dest_ids, gate_fixed, gate_up, down):
    peer_count = lax.axis_size("ep")
    own_rows = tokens[0]
    width = own_rows.shape[1]
    top_count = dest_ids.shape[2]
    gates = gate_fixed[0]
    route_table = jnp.concatenate([dest_ids[0], gates >> 8, gates & 255], axis=1)
    route_pad = jnp.pad(route_table, ((0, 0), (0, 128 - 3 * top_count))).astype(jnp.bfloat16)
    packed = lax.all_gather(
        jnp.concatenate([own_rows, route_pad], axis=1), "dp", axis=0, tiled=True
    )
    column_rows = packed[:, :width]
    table = packed[:, width : width + 3 * top_count].astype(jnp.int32)
    column_table = jnp.concatenate(
        [
            table[:, :top_count],
            table[:, top_count : 2 * top_count] * 256 + table[:, 2 * top_count :],
        ],
        axis=1,
    )
    col_rows = column_table.shape[0]
    capacity = min(col_rows, max(2, 2 * col_rows * top_count // peer_count))
    target_dev = column_table[:, :top_count].reshape(-1)
    gate_raw = column_table[:, top_count:].astype(jnp.float32)
    gate_norm = gate_raw / jnp.sum(gate_raw, axis=1, keepdims=True)
    marks = (target_dev[:, None] == jnp.arange(peer_count, dtype=jnp.int32)[None, :]).astype(
        jnp.int32
    )
    slot_rank = jnp.sum(jnp.cumsum(marks, axis=0) * marks, axis=1) - 1
    slot_index = target_dev * capacity + slot_rank
    source_row = jnp.arange(target_dev.shape[0], dtype=jnp.int32) // top_count
    send_block = (
        jnp.zeros((peer_count * capacity, width), jnp.bfloat16)
        .at[slot_index]
        .set(column_rows[source_row])
        .reshape(peer_count, capacity, width)
    )
    rows = lax.all_to_all(send_block, "ep", split_axis=0, concat_axis=0, tiled=True)
    flat_rows = rows.reshape(-1, rows.shape[2])
    own_out = feed_forward(flat_rows, gate_up[0], down[0])
    returned = lax.all_to_all(
        own_out.reshape(rows.shape[0], rows.shape[1], -1),
        "ep",
        split_axis=0,
        concat_axis=0,
        tiled=True,
    )
    flat_back = returned.reshape(peer_count * capacity, -1)
    weighted = flat_back[slot_index].astype(jnp.float32) * gate_norm.reshape(-1)[:, None]
    summed = jnp.sum(weighted.reshape(col_rows, top_count, -1), axis=1)
    parts = lax.all_to_all(
        summed.astype(jnp.bfloat16).reshape(4, -1, width),
        "dp",
        split_axis=0,
        concat_axis=0,
        tiled=True,
    )
    mine = jnp.sum(parts.astype(jnp.float32), axis=0).astype(jnp.bfloat16)
    return mine[None]


def solution(mesh):
    return jax.shard_map(
        per_device,
        mesh=mesh,
        in_specs=(
            P("ep", "dp", None),
            P("ep", "dp", None),
            P("ep", "dp", None),
            P("ep", None, "dp", None),
            P("ep", "dp", None),
        ),
        out_specs=P("ep", "dp", None),
        check_vma=False,
    )
```

profile of v0, /device:TPU:8, one launch (start us, length us, event | category | flops | bytes accessed | tf_op | source)
XLA Modules:
  0.0 122.4 jit_solution(11102416586996701243)
XLA Ops:
  0.0 0.8 fusion.25
  0.9 0.7 maximum_bitcast_fusion
  1.6 12.2 %all-gather = bf16[4,4,2176]{2,1,0:T(4,128)(2,1)S(1)} all-gather(bf16[1,4,2176]{2,1,0:T(4,128)(2,1)S(1)} %maximum_bitcast_fusion), channel_id=1, replica_groups=mesh['dp'=4,'ep'=128] {'dp'}, dimensions={0}, use_global_device_ids=true | all-gather | bytes 87040 | tf_op jit(solution)/shard_map/all_gather | solution.py:22
  13.9 0.1 eq.15
  14.0 0.1 fusion.19
  14.1 0.2 reduce_window_sum.11
  14.3 0.2 select_reduce_fusion
  14.4 0.1 mul.43
  14.5 3.4 %scatter_custom_fusion = bf16[256,2048]{1,0:T(8,128)(2,1)S(1)} fusion(s32[128]{0:T(128)S(1)} %fusion.30, bf16[16,2048]{1,0:T(8,128)(2,1)S(1)} %slice.36, s32[1024]{0:T(1024)S(1)} %pad_clamp_fusion.1, bf16[]{:T(256)} %constant.33.clone.1), kind=kCustom, calls=%fused_computation.14 | custom fusion | bytes 1048578 | tf_op jit(solution)/shard_map/scatter | solution.py:48
  17.9 0.7 reshape.114
  18.6 48.6 %all_to_all.15 = bf16[128,2,2048]{2,1,0:T(2,128)(2,1)S(1)} all-to-all(bf16[128,2,2048]{2,1,0:T(2,128)(2,1)S(1)} %reshape.114), channel_id=1, replica_groups=mesh['dp'=4,'ep'=128] {'ep'}, dimensions={0} | all-to-all | bytes 2097152 | tf_op jit(solution)/shard_map/all_to_all | solution.py:51
  67.2 0.4 reshape.115
  67.7 1.6 %fusion.5 = f32[256,192]{0,1:T(8,128)S(1)} fusion(bf16[256,2048]{1,0:T(8,128)(2,1)S(1)} %reshape.115, bf16[1,2,192,2048]{3,2,1,0:T(8,128)(2,1)} %param.8), kind=kOutput, calls=%fused_computation.10 | convolution fusion | flops 201326592 | bytes 2031616 | tf_op jit(solution)/shard_map/nd,hd->nh/dot_general | solution.py:8
  69.3 2.6 %convolution_convert_fusion = bf16[256,2048]{1,0:T(8,128)(2,1)S(1)} fusion(bf16[256,2048]{1,0:T(8,128)(2,1)S(1)} %reshape.115, bf16[1,192,2048]{2,1,0:T(8,128)(2,1)S(1)} %copy-done, bf16[1,2,192,2048]{3,2,1,0:T(8,128)(2,1)} %param.8, f32[256,192]{0,1:T(8,128)S(1)} %fusion.5), kind=kOutput, calls=%fused_computation.3 | convolution fusion | flops 403472384 | bytes 3866624 | tf_op jit(solution)/shard_map/dot_general | solution.py:11
  71.9 1.5 %reshape.116 = bf16[128,2,2048]{2,1,0:T(2,128)(2,1)} reshape(bf16[256,2048]{1,0:T(8,128)(2,1)S(1)} %convolution_convert_fusion) | data formatting | bytes 2097152 | tf_op jit(solution)/shard_map/reshape | solution.py:55
  73.4 5.9 %all-to-all-start.1 = ((bf16[128,2,2048]{2,1,0:T(2,128)(2,1)}), bf16[128,2,2048]{2,1,0:T(2,128)(2,1)S(1)}, u32[]{:S(2)}, u32[]{:S(2)}) async-start(bf16[128,2,2048]{2,1,0:T(2,128)(2,1)} %reshape.116), calls=%async_computation.1 | async-start | bytes 2097152 | tf_op jit(solution)/shard_map/all_to_all | solution.py:54
  79.4 0.2 fusion.21
  79.6 0.1 broadcast_divide_fusion
  79.6 31.2 %all-to-all-done.1 = bf16[128,2,2048]{2,1,0:T(2,128)(2,1)S(1)} async-done(((bf16[128,2,2048]{2,1,0:T(2,128)(2,1)}), bf16[128,2,2048]{2,1,0:T(2,128)(2,1)S(1)}, u32[]{:S(2)}, u32[]{:S(2)}) %all-to-all-start.1) | async-done | bytes 1048608 | tf_op jit(solution)/shard_map/all_to_all | solution.py:54
  110.8 0.4 reshape.117
  111.2 0.9 gather_fusion
  112.2 0.5 fusion.1
  112.7 9.1 %all_to_all.16 = bf16[4,4,2048]{2,1,0:T(4,128)(2,1)S(1)} all-to-all(bf16[4,4,2048]{2,1,0:T(4,128)(2,1)S(1)} %convert_element_type.40), channel_id=1, replica_groups=mesh['dp'=4,'ep'=128] {'dp'}, dimensions={0} | all-to-all | bytes 131072 | tf_op jit(solution)/shard_map/all_to_all | solution.py:64
  121.8 0.6 reduce_sum.42
  (12 shorter events, 0.2 us)
Async XLA Ops:
  0.0 69.3 %copy-start = (bf16[1,192,2048]{2,1,0:T(8,128)(2,1)S(1)}, bf16[1,192,2048]{2,1,0:T(8,128)(2,1)}, u32[]{:S(2)}) copy-start(bf16[1,192,2048]{2,1,0:T(8,128)(2,1)} %param.9) | copy-start | bytes 2359300
  73.4 37.4 %all-to-all-start.1 = ((bf16[128,2,2048]{2,1,0:T(2,128)(2,1)}), bf16[128,2,2048]{2,1,0:T(2,128)(2,1)S(1)}, u32[]{:S(2)}, u32[]{:S(2)}) async-start(bf16[128,2,2048]{2,1,0:T(2,128)(2,1)} %reshape.116), calls=%async_computation.1 | async-start | bytes 2097152 | tf_op jit(solution)/shard_map/all_to_all | solution.py:54
where the time goes:
time: 123 us; the launch traced here: 122 us
  blocking collectives  69.9 us (57%)
  waiting for transfers between devices  31.2 us (25%)
  local copies, waits for them, and re-layouts  7.6 us (6%)
  starting transfers between devices  5.94 us (5%)
  matrix products  4.2 us (3%)
  other arithmetic  3.41 us (3%)
    all_to_all x1, blocking collectives, per_device(): lax.all_to_all(send_block, 'ep', split_axis=0, concat_axis=0, tiled=True)  48.6 us
    all_to_all x1, waiting for transfers between devices, per_device(): lax.all_to_all(own_out.reshape(rows.shape[0], rows.shape[1], -1), 'ep', s...  31.2 us
    all_gather x1, blocking collectives, per_device(): lax.all_gather(jnp.concatenate([own_rows, route_pad], axis=1), 'dp', axis...  12.2 us
    all_to_all x1, blocking collectives, per_device(): lax.all_to_all(summed.astype(jnp.bfloat16).reshape(4, -1, width), 'dp', s...  9.09 us
    all_to_all x1, starting transfers between devices, per_device(): lax.all_to_all(own_out.reshape(rows.shape[0], rows.shape[1], -1), 'ep', s...  5.94 us
    scatter x1, local copies, waits for them, and re-layouts, per_device(): send_block = jnp.zeros((peer_count * capacity, width), jnp.bfloat16).at[s...  3.36 us
    dot_general x1, matrix products, feed_forward(): jnp.dot(hidden, lower, preferred_element_type=jnp.float32)  2.57 us
  transfers between devices with their start and end apart: 1, of which 1 were waited for; matrix products, arithmetic and copies ran while one was open for 0% of the time, Pallas kernels for 0%

commit v1 on v0

--- a/solution.py
+++ b/solution.py
@@ -2,6 +2,28 @@
 import jax.numpy as jnp
 from jax import lax
 from jax.sharding import PartitionSpec as P
+
+
+def laid_out(blocks, dim):
+    blocks = jnp.moveaxis(blocks, 0, dim)
+    shape = blocks.shape
+    return blocks.reshape(*shape[:dim], shape[dim] * shape[dim + 1], *shape[dim + 2 :])
+
+
+def ring_gather(value, axis, dim):
+    size = lax.axis_size(axis)
+    pairs = [(i, (i + 1) % size) for i in range(size)]
+    back = [(b, a) for a, b in pairs]
+    lower, upper = ([], [])
+    for step in range(size - 1):
+        if step % 2 == 0:
+            lower.append(lax.ppermute(lower[-1] if lower else value, axis, pairs))
+        else:
+            upper.append(lax.ppermute(upper[-1] if upper else value, axis, back))
+    parts = jnp.stack([*lower[::-1], value, *upper])
+    shift = lax.axis_index(axis) - len(lower)
+    parts = parts[(jnp.arange(size) - shift) % size]
+    return laid_out(parts, dim)
 
 
 def feed_forward(rows, pair, lower):
@@ -19,9 +41,7 @@
     gates = gate_fixed[0]
     route_table = jnp.concatenate([dest_ids[0], gates >> 8, gates & 255], axis=1)
     route_pad = jnp.pad(route_table, ((0, 0), (0, 128 - 3 * top_count))).astype(jnp.bfloat16)
-    packed = lax.all_gather(
-        jnp.concatenate([own_rows, route_pad], axis=1), "dp", axis=0, tiled=True
-    )
+    packed = ring_gather(jnp.concatenate([own_rows, route_pad], axis=1), "dp", 0)
     column_rows = packed[:, :width]
     table = packed[:, width : width + 3 * top_count].astype(jnp.int32)
     column_table = jnp.concatenate(

time: 123 us -> 124 us (level)
  blocking collectives: 69.9 us -> 56.6 us
  starting transfers between devices: 5.94 us -> 15.2 us
  waiting for transfers between devices: 31.2 us -> 35.8 us
    all_gather x1 -> x0, blocking collectives: 12.2 us -> none  [per_device(): lax.all_gather(jnp.concatenate([own_rows, route_pad], axis=1), 'dp', axis...]
    ppermute x0 -> x3, starting transfers between devices: none -> 9.24 us  [the longest x2 5.59 us: ring_gather(): lower.append(lax.ppermute(lower[-1] if lower else value, axis, pairs))]
    ppermute x0 -> x3, waiting for transfers between devices: none -> 4.64 us  [the longest x2 4.64 us: ring_gather(): lower.append(lax.ppermute(lower[-1] if lower else value, axis, pairs))]
  transfers between devices with their start and end apart: 1 -> 4, of which waited for: 1 -> 2; matrix products, arithmetic and copies ran while one was open for 0% -> 0% of each run, Pallas kernels for 0% -> 0%
where the time goes in v1:
time: 124 us
  blocking collectives  56.6 us (46%)
  waiting for transfers between devices  35.8 us (29%)
  starting transfers between devices  15.2 us (12%)
  local copies, waits for them, and re-layouts  8.22 us (7%)
  matrix products  4.21 us (3%)
  other arithmetic  3.49 us (3%)
    all_to_all x1, blocking collectives, per_device(): lax.all_to_all(send_block, 'ep', split_axis=0, concat_axis=0, tiled=True)  48.6 us
    all_to_all x1, waiting for transfers between devices, per_device(): lax.all_to_all(own_out.reshape(rows.shape[0], rows.shape[1], -1), 'ep', s...  31.2 us
    all_to_all x1, blocking collectives, per_device(): lax.all_to_all(summed.astype(jnp.bfloat16).reshape(4, -1, width), 'dp', s...  7.99 us
    all_to_all x1, starting transfers between devices, per_device(): lax.all_to_all(own_out.reshape(rows.shape[0], rows.shape[1], -1), 'ep', s...  5.93 us
    ppermute x2, starting transfers between devices, ring_gather(): lower.append(lax.ppermute(lower[-1] if lower else value, axis, pairs))  5.59 us
    ppermute x2, waiting for transfers between devices, ring_gather(): lower.append(lax.ppermute(lower[-1] if lower else value, axis, pairs))  4.64 us
    ppermute x1, starting transfers between devices, ring_gather(): upper.append(lax.ppermute(upper[-1] if upper else value, axis, back))  3.65 us
    scatter x1, local copies, waits for them, and re-layouts, per_device(): send_block = jnp.zeros((peer_count * capacity, width), jnp.bfloat16).at[s...  3.36 us
  transfers between devices with their start and end apart: 4, of which 2 were waited for; matrix products, arithmetic and copies ran while one was open for 0% of the time, Pallas kernels for 0%

profile of v1, /device:TPU:8, one launch (start us, length us, event | category | flops | bytes accessed | tf_op | source)
XLA Modules:
  0.0 123.7 jit_solution(13121722479312869379)
XLA Ops:
  0.0 0.8 fusion.25
  0.9 0.7 fusion.34
  1.6 3.4 %collective-permute-start = (bf16[4,2176]{1,0:T(4,128)(2,1)S(1)}, bf16[4,2176]{1,0:T(4,128)(2,1)S(1)}, u32[]{:S(2)}, u32[]{:S(2)}) collective-permute-start(bf16[4,2176]{1,0:T(4,128)(2,1)S(1)} %get-tuple-element.6), channel_id=1, source_target_pairs={{0,128},{128,256},{256,384},{384,0},{1,129},{129,257},{257,385},{3... | collective-permute-start | bytes 52232 | tf_op jit(solution)/shard_map/ppermute | solution.py:20
  5.0 3.7 %collective-permute-start.2 = (bf16[4,2176]{1,0:T(4,128)(2,1)S(1)}, bf16[4,2176]{1,0:T(4,128)(2,1)S(1)}, u32[]{:S(2)}, u32[]{:S(2)}) collective-permute-start(bf16[4,2176]{1,0:T(4,128)(2,1)S(1)} %get-tuple-element.6), channel_id=1, source_target_pairs={{128,0},{256,128},{384,256},{0,384},{129,1},{257,129},{385,257},{1... | collective-permute-start | bytes 52232 | tf_op jit(solution)/shard_map/ppermute | solution.py:22
  8.7 2.2 %collective-permute-start.1 = (bf16[4,2176]{1,0:T(4,128)(2,1)S(1)}, bf16[4,2176]{1,0:T(4,128)(2,1)S(1)}, u32[]{:S(2)}, u32[]{:S(2)}) collective-permute-start(bf16[4,2176]{1,0:T(4,128)(2,1)S(1)} %collective-permute-done), channel_id=1, source_target_pairs={{0,128},{128,256},{256,384},{384,0},{1,129},{129,257},{257,385},{3... | collective-permute-start | bytes 52232 | tf_op jit(solution)/shard_map/ppermute | solution.py:20
  10.9 4.6 %collective-permute-done.1 = bf16[4,2176]{1,0:T(4,128)(2,1)S(1)} collective-permute-done((bf16[4,2176]{1,0:T(4,128)(2,1)S(1)}, bf16[4,2176]{1,0:T(4,128)(2,1)S(1)}, u32[]{:S(2)}, u32[]{:S(2)}) %collective-permute-start.1) | collective-permute-done | bytes 17440 | tf_op jit(solution)/shard_map/ppermute | solution.py:20
  15.6 0.6 gather_fusion
  16.5 0.2 reduce_window_sum.11
  16.7 0.2 select_reduce_fusion
  17.0 3.4 %scatter_custom_fusion = bf16[256,2048]{1,0:T(8,128)(2,1)S(1)} fusion(s32[128]{0:T(128)S(1)} %fusion.32, bf16[16,2048]{1,0:T(8,128)(2,1)S(1)} %slice.38, s32[1024]{0:T(1024)S(1)} %pad_clamp_fusion.1, bf16[]{:T(256)} %constant.53.clone.1), kind=kCustom, calls=%fused_computation.15 | custom fusion | bytes 1048578 | tf_op jit(solution)/shard_map/scatter | solution.py:68
  20.3 0.7 reshape.167
  21.0 48.6 %all_to_all.15 = bf16[128,2,2048]{2,1,0:T(2,128)(2,1)S(1)} all-to-all(bf16[128,2,2048]{2,1,0:T(2,128)(2,1)S(1)} %reshape.167), channel_id=1, replica_groups=mesh['dp'=4,'ep'=128] {'ep'}, dimensions={0} | all-to-all | bytes 2097152 | tf_op jit(solution)/shard_map/all_to_all | solution.py:71
  69.7 0.4 reshape.168
  70.1 1.6 %fusion.5 = f32[256,192]{0,1:T(8,128)S(1)} fusion(bf16[256,2048]{1,0:T(8,128)(2,1)S(1)} %reshape.168, bf16[1,2,192,2048]{3,2,1,0:T(8,128)(2,1)} %param.8), kind=kOutput, calls=%fused_computation.11 | convolution fusion | flops 201326592 | bytes 2031616 | tf_op jit(solution)/shard_map/nd,hd->nh/dot_general | solution.py:30
  71.7 2.6 %convolution_convert_fusion = bf16[256,2048]{1,0:T(8,128)(2,1)S(1)} fusion(bf16[256,2048]{1,0:T(8,128)(2,1)S(1)} %reshape.168, bf16[1,192,2048]{2,1,0:T(8,128)(2,1)S(1)} %copy-done, bf16[1,2,192,2048]{3,2,1,0:T(8,128)(2,1)} %param.8, f32[256,192]{0,1:T(8,128)S(1)} %fusion.5), kind=kOutput, calls=%fused_computation.4 | convolution fusion | flops 403472384 | bytes 3866624 | tf_op jit(solution)/shard_map/dot_general | solution.py:33
  74.3 1.5 %reshape.169 = bf16[128,2,2048]{2,1,0:T(2,128)(2,1)} reshape(bf16[256,2048]{1,0:T(8,128)(2,1)S(1)} %convolution_convert_fusion) | data formatting | bytes 2097152 | tf_op jit(solution)/shard_map/reshape | solution.py:75
  75.8 5.9 %all-to-all-start.1 = ((bf16[128,2,2048]{2,1,0:T(2,128)(2,1)}), bf16[128,2,2048]{2,1,0:T(2,128)(2,1)S(1)}, u32[]{:S(2)}, u32[]{:S(2)}) async-start(bf16[128,2,2048]{2,1,0:T(2,128)(2,1)} %reshape.169), calls=%async_computation.1 | async-start | bytes 2097152 | tf_op jit(solution)/shard_map/all_to_all | solution.py:74
  81.8 0.2 fusion.21
  82.0 31.2 %all-to-all-done.1 = bf16[128,2,2048]{2,1,0:T(2,128)(2,1)S(1)} async-done(((bf16[128,2,2048]{2,1,0:T(2,128)(2,1)}), bf16[128,2,2048]{2,1,0:T(2,128)(2,1)S(1)}, u32[]{:S(2)}, u32[]{:S(2)}) %all-to-all-start.1) | async-done | bytes 1048608 | tf_op jit(solution)/shard_map/all_to_all | solution.py:74
  113.2 0.4 reshape.170
  113.6 0.9 gather_fusion.1
  114.6 0.5 fusion.1
  115.1 8.0 %all_to_all.16 = bf16[4,4,2048]{2,1,0:T(4,128)(2,1)S(1)} all-to-all(bf16[4,4,2048]{2,1,0:T(4,128)(2,1)S(1)} %convert_element_type.40), channel_id=1, replica_groups=mesh['dp'=4,'ep'=128] {'dp'}, dimensions={0} | all-to-all | bytes 131072 | tf_op jit(solution)/shard_map/all_to_all | solution.py:84
  123.1 0.6 reduce_sum.42
  (21 shorter events, 0.6 us)
Async XLA Ops:
  0.0 71.7 %copy-start = (bf16[1,192,2048]{2,1,0:T(8,128)(2,1)S(1)}, bf16[1,192,2048]{2,1,0:T(8,128)(2,1)}, u32[]{:S(2)}) copy-start(bf16[1,192,2048]{2,1,0:T(8,128)(2,1)} %param.9) | copy-start | bytes 2359300
  1.6 7.1 %collective-permute-start = (bf16[4,2176]{1,0:T(4,128)(2,1)S(1)}, bf16[4,2176]{1,0:T(4,128)(2,1)S(1)}, u32[]{:S(2)}, u32[]{:S(2)}) collective-permute-start(bf16[4,2176]{1,0:T(4,128)(2,1)S(1)} %get-tuple-element.6), channel_id=1, source_target_pairs={{0,128},{128,256},{256,384},{384,0},{1,129},{129,257},{257,385},{3... | collective-permute-start | bytes 52232 | tf_op jit(solution)/shard_map/ppermute | solution.py:20
  5.0 5.9 %collective-permute-start.2 = (bf16[4,2176]{1,0:T(4,128)(2,1)S(1)}, bf16[4,2176]{1,0:T(4,128)(2,1)S(1)}, u32[]{:S(2)}, u32[]{:S(2)}) collective-permute-start(bf16[4,2176]{1,0:T(4,128)(2,1)S(1)} %get-tuple-element.6), channel_id=1, source_target_pairs={{128,0},{256,128},{384,256},{0,384},{129,1},{257,129},{385,257},{1... | collective-permute-start | bytes 52232 | tf_op jit(solution)/shard_map/ppermute | solution.py:22
  8.7 6.9 %collective-permute-start.1 = (bf16[4,2176]{1,0:T(4,128)(2,1)S(1)}, bf16[4,2176]{1,0:T(4,128)(2,1)S(1)}, u32[]{:S(2)}, u32[]{:S(2)}) collective-permute-start(bf16[4,2176]{1,0:T(4,128)(2,1)S(1)} %collective-permute-done), channel_id=1, source_target_pairs={{0,128},{128,256},{256,384},{384,0},{1,129},{129,257},{257,385},{3... | collective-permute-start | bytes 52232 | tf_op jit(solution)/shard_map/ppermute | solution.py:20
  75.8 37.4 %all-to-all-start.1 = ((bf16[128,2,2048]{2,1,0:T(2,128)(2,1)}), bf16[128,2,2048]{2,1,0:T(2,128)(2,1)S(1)}, u32[]{:S(2)}, u32[]{:S(2)}) async-start(bf16[128,2,2048]{2,1,0:T(2,128)(2,1)} %reshape.169), calls=%async_computation.1 | async-start | bytes 2097152 | tf_op jit(solution)/shard_map/all_to_all | solution.py:74
